TPU v7x, 128 devices: a whole 4x4x4 slice. The times are simulated.
128 devices in a mesh: front: 8 (over z, core), grid: 16 (over y, x).
Axes of the slice: x: 4, y: 4, z: 4, core: 2. Of those that a mesh axis runs over, the one named last changes fastest.
Arguments:
- pivot_block: float32 [8, 512, 512], P('front'), as said below
- border: float32 [8, 8192, 512], P('front', 'grid'), may hold values from -0.9 to 0.9
- trailing: float32 [8, 8192, 8192], P('front', 'grid'), as said below
- dest_owner: int32 [8, 2560, 1], P('front', 'grid'), may hold values from 0 to 127; in each aligned block of 160 rows (0 to 159, 160 to 319, ..., all dimensions but the last counted through in order) at most 2 rows name the same one
- dest_slot: int32 [8, 2560], P('front', 'grid'), may hold values from 0 to 63
- row_map: int32 [8, 2560, 128], P('front', 'grid'), may hold values from 0 to 127, each once within a row
Outputs:
- pivot_factor: float32 [8, 512, 512], P('front')
- border_factor: float32 [8, 8192, 512], P('front', 'grid')
- ancestor_blocks: float32 [8192, 128, 128], P(('front', 'grid'))
Inputs may be any that keep to these rules, and one draw needn't show every extreme that they name: `pivot_block`: symmetric positive definite. `trailing`: Symmetric. `dest_owner`: in each aligned block of 160 entries no owner is named more than 2 times, a bound that some block reaches.
All inputs are finite; a program needn't handle non-finite values.
Results may differ from a plain program's by a relative error of at most 0.0001.
Values sent between devices are 32-bit elements; how exact they have to be, the bound alone decides.
A program may use at most 192 MiB of HBM per device.

v0:
```python
import jax
import jax.numpy as jnp
from jax import lax
from jax.sharding import PartitionSpec as P

BLK = 128
NB = 256
SLOTS = 64
precise = lax.Precision.HIGHEST


def factor_panels(corner, border_rows_in):
    first_factor = jnp.linalg.cholesky(corner[:NB, :NB])
    remainder = jnp.concatenate([corner[NB:, :NB], border_rows_in[:, :NB]], axis=0)
    solved = jax.scipy.linalg.solve_triangular(first_factor, remainder.T, lower=True).T
    pivot_rows = solved[:NB]
    border_rows = solved[NB:]
    updated_pivot = corner[NB:, NB:] - jnp.dot(pivot_rows, pivot_rows.T, precision=precise)
    updated_border = border_rows_in[:, NB:] - jnp.dot(border_rows, pivot_rows.T, precision=precise)
    second_factor = jnp.linalg.cholesky(updated_pivot)
    second_border = jax.scipy.linalg.solve_triangular(second_factor, updated_border.T, lower=True).T
    upper_half = jnp.concatenate([first_factor, jnp.zeros((NB, NB), jnp.float32)], axis=1)
    lower_half = jnp.concatenate([pivot_rows, second_factor], axis=1)
    return (
        jnp.concatenate([upper_half, lower_half], axis=0),
        jnp.concatenate([border_rows, second_border], axis=1),
    )


def subtract_outer(base_rows, left_rows, piece):
    return base_rows - jnp.einsum("rk,ck->rc", left_rows, piece, precision=precise)


def body(pivot_block, border, trailing, dest_owner, dest_slot, row_map):
    pivot_factor, border_factor = factor_panels(pivot_block[0], border[0])
    local_rows = trailing[0]
    schur_rows = local_rows
    for column_start in (0, NB):
        panel_cols = border_factor[:, column_start : column_start + NB]
        schur_rows = subtract_outer(
            schur_rows, panel_cols, lax.all_gather(panel_cols, "grid", axis=0, tiled=True)
        )
    group_size = lax.axis_size("grid")
    member = lax.axis_index("grid")
    per_dev = local_rows.shape[0] // BLK
    blocks_all = local_rows.shape[1] // BLK
    listed = dest_owner.shape[1]
    candidates = jnp.arange(per_dev * blocks_all, dtype=jnp.int32)
    local_block = candidates // blocks_all
    column_block = candidates % blocks_all
    true_column = column_block % per_dev * group_size + column_block // per_dev
    true_row = local_block * group_size + member
    usable = true_column <= true_row
    position = jnp.cumsum(usable.astype(jnp.int32)) - 1
    matches = (
        usable[None, :] & (position[None, :] == jnp.arange(listed, dtype=jnp.int32)[:, None])
    ).astype(jnp.float32)
    front_count = lax.axis_size("front")
    devices = front_count * group_size
    capacity = max(2, (listed + devices - 1) // devices)
    owner_id = dest_owner[0, :, 0]
    owner_hits = (owner_id[:, None] == jnp.arange(devices, dtype=jnp.int32)[None, :]).astype(
        jnp.int32
    )
    earlier = jnp.cumsum(owner_hits, axis=0) - owner_hits
    rank_in = jnp.sum(earlier * owner_hits, axis=1)
    buffer_place = owner_id * capacity + rank_in
    slot_hits = buffer_place[None, :] == jnp.arange(devices * capacity, dtype=jnp.int32)[:, None]
    sender = jnp.sum(
        slot_hits.astype(jnp.int32) * jnp.arange(listed, dtype=jnp.int32)[None, :], axis=1
    )
    filled = jnp.any(slot_hits, axis=1)
    selector = jnp.dot(slot_hits.astype(jnp.float32), matches, precision=precise)
    selector = selector.reshape(devices * capacity, per_dev, blocks_all)
    blocked = schur_rows.reshape(per_dev, BLK, blocks_all, BLK)
    picked = jnp.einsum("qkc,krcs->qrs", selector, blocked, precision=precise)
    row_order = row_map[0][sender]
    permuter = (row_order[:, :, None] == jnp.arange(BLK, dtype=jnp.int32)[None, None, :]).astype(
        jnp.float32
    )
    moved = jnp.einsum("qrs,qsx->qrx", permuter, picked, precision=precise)
    outgoing = moved.reshape(devices, capacity, BLK * BLK)
    slot_out = jnp.where(filled, dest_slot[0][sender], 0).reshape(devices, capacity)
    arrived, slot_in = (
        lax.all_to_all(outgoing, ("front", "grid"), split_axis=0, concat_axis=0, tiled=True),
        lax.all_to_all(slot_out, ("front", "grid"), split_axis=0, concat_axis=0, tiled=True),
    )
    arrived = arrived.reshape(devices * capacity, BLK * BLK)
    slot_in = slot_in.reshape(devices * capacity)
    chooser = (slot_in[:, None] == jnp.arange(SLOTS, dtype=jnp.int32)[None, :]).astype(jnp.float32)
    summed = jnp.einsum("rs,rx->sx", chooser, arrived, precision=precise)
    return (pivot_factor[None], border_factor[None], summed.reshape(SLOTS, BLK, BLK))


def solution(mesh):
    return jax.shard_map(
        body,
        mesh=mesh,
        in_specs=(
            P("front", None, None),
            P("front", "grid", None),
            P("front", "grid", None),
            P("front", "grid", None),
            P("front", "grid"),
            P("front", "grid", None),
        ),
        out_specs=(
            P("front", None, None),
            P("front", "grid", None),
            P(("front", "grid"), None, None),
        ),
        check_vma=False,
    )
```

profile of v0, /device:TPU:5, one launch (start us, length us, event | category | flops | bytes accessed | tf_op | source)
XLA Modules:
  0.0 670.3 jit_solution(7392036229213009177)
XLA Ops:
  7.3 1.6 copy.53
  9.1 11.7 %cholesky.130 = f32[128,128]{1,0:T(8,128)S(1)} custom-call(f32[128,128]{1,0:T(8,128)S(1)} %cholesky.194), custom_call_target="Cholesky" | custom-call | tf_op jit(solution)/shard_map/jit(cholesky)/cholesky | solution.py:13
  20.8 9.8 %custom-call.19 = f32[1,128,128]{1,2,0:T(8,128)S(1)} custom-call(f32[1,128,128]{2,1,0:T(8,128)S(1)} %get-tuple-element.65), custom_call_target="InvertDiagBlocksLowerTriangular" | custom-call | tf_op jit(solution)/shard_map/jit(cholesky)/cholesky | solution.py:13
  31.1 11.7 %cholesky.147 = f32[128,128]{1,0:T(8,128)S(1)} custom-call(f32[128,128]{1,0:T(8,128)S(1)} %convolution_subtract_fusion.5), custom_call_target="Cholesky" | custom-call | tf_op jit(solution)/shard_map/jit(cholesky)/cholesky | solution.py:13
  42.9 0.6 compare_reduce_fusion.2
  44.8 0.7 fusion.20
  45.7 4.3 while.2
  46.5 1.4 bitcast_dynamic-update-slice_fusion.4
  48.5 1.4 bitcast_dynamic-update-slice_fusion.4
  49.9 19.7 %custom-call.16 = f32[2,128,128]{1,2,0:T(8,128)S(1)} custom-call(f32[2,128,128]{2,1,0:T(8,128)S(1)} %get-tuple-element.11), custom_call_target="InvertDiagBlocksLowerTriangular" | custom-call | tf_op jit(solution)/shard_map/jit(_solve_triangular)/triangular_solve | solution.py:15
  69.6 1.6 copy.55
  72.3 0.9 copy.56
  73.2 0.8 fusion.37
  74.0 1.1 maximum_bitcast_fusion.2
  75.1 0.8 slice.133
  76.6 11.7 %cholesky.164 = f32[128,128]{1,0:T(8,128)S(1)} custom-call(f32[128,128]{1,0:T(8,128)S(1)} %cholesky.197), custom_call_target="Cholesky" | custom-call | tf_op jit(solution)/shard_map/jit(cholesky)/cholesky | solution.py:20
  88.4 9.8 %custom-call.20 = f32[1,128,128]{1,2,0:T(8,128)S(1)} custom-call(f32[1,128,128]{2,1,0:T(8,128)S(1)} %get-tuple-element.61), custom_call_target="InvertDiagBlocksLowerTriangular" | custom-call | tf_op jit(solution)/shard_map/jit(cholesky)/cholesky | solution.py:20
  98.9 11.7 %cholesky.181 = f32[128,128]{1,0:T(8,128)S(1)} custom-call(f32[128,128]{1,0:T(8,128)S(1)} %convolution_subtract_fusion.4), custom_call_target="Cholesky" | custom-call | tf_op jit(solution)/shard_map/jit(cholesky)/cholesky | solution.py:20
  110.7 0.6 compare_reduce_fusion
  111.3 0.6 compare_reduce_fusion.1
  113.2 12.1 %while.3 = (s32[]{:T(128)}, f32[256,256]{1,0:T(8,128)S(1)}, s32[2,2]{1,0:T(2,128)S(1)}, f32[2,128,128]{2,1,0:T(8,128)S(1)}, s32[]{:T(128)}) while((s32[]{:T(128)}, f32[256,256]{1,0:T(8,128)S(1)}, s32[2,2]{1,0:T(2,128)S(1)}, f32[2,128,128]{2,1,0:T(8,128)S(1)}, s32[]{:T(128)}) %tuple.61), condition=%wide.while_cond.1, body=%wide.while_body.1.sunk | while | flops 2 | bytes 131181 | solution.py:21
  121.5 0.6 fusion.77
  122.1 1.3 bitcast_dynamic-update-slice_fusion.5
  124.0 1.3 bitcast_dynamic-update-slice_fusion.5
  125.3 19.7 %custom-call.17 = f32[2,128,128]{1,2,0:T(8,128)S(1)} custom-call(f32[2,128,128]{2,1,0:T(8,128)S(1)} %get-tuple-element.19), custom_call_target="InvertDiagBlocksLowerTriangular" | custom-call | tf_op jit(solution)/shard_map/jit(_solve_triangular)/triangular_solve | solution.py:21
  145.0 0.6 fusion.10
  146.6 1.4 fusion.33
  148.0 0.8 fusion.12
  149.6 1.9 gather_fusion
  151.6 0.8 select_n.78
  152.4 10.8 %all-to-all-start = ((s32[128,1,2]{2,1,0:T(1,128)}), s32[128,1,2]{2,1,0:T(1,128)S(1)}, u32[]{:S(2)}, u32[]{:S(2)}) async-start(s32[128,1,2]{2,1,0:T(1,128)} %bitcast.26), calls=%async_computation | async-start | bytes 131072 | tf_op jit(solution)/shard_map/all_to_all | solution.py:86
  163.7 0.7 gather_fusion.1
  165.0 18.5 %fusion.56 = f32[512,8192]{1,0:T(8,128)} fusion(f32[8192,256]{1,0:T(8,128)} %all-gather.3.cloned.1.call-done, f32[768,256]{1,0:T(8,128)S(1)} %maximum_bitcast_fusion.2), kind=kOutput, calls=%fused_computation.134 | convolution fusion | flops 12884901888 | bytes 25690112 | tf_op jit(solution)/shard_map/rk,ck->rc/dot_general | solution.py:31
  183.5 39.6 %all-gather.5.cloned.1.call-done = f32[8192,256]{1,0:T(8,128)} async-done(((f32[512,256]{1,0:T(8,128)}), f32[8192,256]{1,0:T(8,128)}) %all-gather.5.cloned.1.call-update) | async-done | bytes 8388624 | tf_op jit(solution)/shard_map/all_gather | solution.py:41
  223.1 42.1 %fusion.3 = f32[64,8,64,128]{3,1,2,0:T(8,128)} fusion(f32[512,8192]{1,0:T(8,128)} %fusion.56, f32[1,512,8192]{2,1,0:T(8,128)} %param.9, f32[8192,256]{1,0:T(8,128)} %all-gather.5.cloned.1.call-done, f32[128,512]{0,1:T(8,128)S(1)} %fusion.33, f32[128,512]{0,1:T(8,128)S(1)} %copy.62), kind=kOutput, calls=%fused_computation.10 | convolution fusion | flops 12893421568 | bytes 59244544 | tf_op jit(solution)/shard_map/rk,ck->rc/dot_general | solution.py:31
  265.2 14.1 %copy.76 = f32[64,8,64,128]{3,2,1,0:T(8,128)} copy(f32[64,8,64,128]{3,1,2,0:T(8,128)} %fusion.3) | data formatting | bytes 33554432
  279.3 18.7 %fusion.6 = f32[256,128,128]{2,0,1:T(8,128)S(1)} fusion(f32[256,4,64,1]{0,2,3,1:T(8,128)S(1)} %bitcast.140, f32[4,128,64,128]{3,2,1,0:T(8,128)} %bitcast.130), kind=kOutput, calls=%fused_computation.14 | convolution fusion | flops 12884901888 | bytes 33816576 | tf_op jit(solution)/shard_map/qkc,krcs->qrs/dot_general | solution.py:76
  298.0 26.6 %fusion.4 = f32[256,128,128]{2,1,0:T(8,128)} fusion(f32[256,128,128]{2,0,1:T(8,128)S(1)} %fusion.6, s32[256,128]{1,0:T(8,128)S(1)} %gather_fusion.1), kind=kOutput, calls=%fused_computation.11 | convolution fusion | flops 6446645248 | bytes 33685504 | tf_op jit(solution)/shard_map/qrs,qsx->qrx/dot_general | solution.py:81
  324.6 19.8 %reshape.216 = f32[128,2,16384]{2,1,0:T(2,128)} reshape(f32[256,128,128]{2,1,0:T(8,128)} %fusion.4) | data formatting | bytes 33554432 | tf_op jit(solution)/shard_map/reshape | solution.py:82
  344.4 9.2 %all-to-all-start.1 = ((f32[128,2,16384]{2,1,0:T(2,128)}), f32[128,2,16384]{2,1,0:T(2,128)}, u32[]{:S(2)}, u32[]{:S(2)}) async-start(f32[128,2,16384]{2,1,0:T(2,128)} %reshape.216), calls=%async_computation.1 | async-start | bytes 33554432 | tf_op jit(solution)/shard_map/all_to_all | solution.py:85
  353.6 1.1 maximum_bitcast_fusion
  354.7 1.1 fusion.11
  356.4 0.8 reduce.13
  357.3 251.7 %all-to-all-done.1 = f32[128,2,16384]{2,1,0:T(2,128)} async-done(((f32[128,2,16384]{2,1,0:T(2,128)}), f32[128,2,16384]{2,1,0:T(2,128)}, u32[]{:S(2)}, u32[]{:S(2)}) %all-to-all-start.1) | async-done | bytes 16777248 | tf_op jit(solution)/shard_map/all_to_all | solution.py:85
  609.0 20.5 %reshape.217 = f32[256,16384]{1,0:T(8,128)} reshape(f32[128,2,16384]{2,1,0:T(2,128)} %all-to-all-done.1) | data formatting | bytes 33554432 | tf_op jit(solution)/shard_map/reshape | solution.py:88
  629.5 17.5 %copy.69 = f32[256,16384]{0,1:T(8,128)} copy(f32[256,16384]{1,0:T(8,128)} %reshape.217) | data formatting | bytes 33554432 | tf_op jit(solution)/shard_map/reshape | solution.py:88
  647.0 11.5 %fusion.43 = f32[64,128,128]{2,0,1:T(8,128)S(1)} fusion(f32[128,128,256]{2,1,0:T(8,128)} %bitcast.129, s32[256]{0:T(256)S(1)} %eq.86), kind=kOutput, calls=%fused_computation.86 | convolution fusion | flops 3221241856 | bytes 20972544 | tf_op jit(solution)/shard_map/rs,rx->sx/dot_general | solution.py:91
  658.5 4.4 copy.70
  (88 shorter events, 8.6 us)
Async XLA Ops:
  7.2 156.5 %copy-start = (s32[1,160,128]{2,1,0:T(8,128)S(1)}, s32[1,160,128]{2,1,0:T(8,128)}, u32[]{:S(2)}) copy-start(s32[1,160,128]{2,1,0:T(8,128)} %param.12) | copy-start | bytes 245764
  7.2 141.7 %copy-start.7 = (s32[1,160,1]{1,2,0:T(1,128)S(1)}, s32[1,160,1]{1,2,0:T(1,128)}, u32[]{:S(2)}) copy-start(s32[1,160,1]{1,2,0:T(1,128)} %param.10) | copy-start | bytes 1924
  7.2 142.4 %copy-start.2 = (s32[1,160]{1,0:T(1,128)S(1)}, s32[1,160]{1,0:T(1,128)}, u32[]{:S(2)}) copy-start(s32[1,160]{1,0:T(1,128)} %param.11) | copy-start | bytes 1924
  7.2 157.7 %all-gather.3.cloned.1.call-start = ((), (), s32[]{:S(2)}) async-start(), calls=%async_computation.2 | async-start | bytes 8912896 | tf_op jit(solution)/shard_map/all_gather | solution.py:41
  76.0 147.1 %all-gather.5.cloned.1.call-start = ((), (), s32[]{:S(2)}) async-start(), calls=%async_computation.3 | async-start | bytes 8912896 | tf_op jit(solution)/shard_map/all_gather | solution.py:41
  145.0 0.7 copy-start.6
  152.4 192.0 %all-to-all-start = ((s32[128,1,2]{2,1,0:T(1,128)}), s32[128,1,2]{2,1,0:T(1,128)S(1)}, u32[]{:S(2)}, u32[]{:S(2)}) async-start(s32[128,1,2]{2,1,0:T(1,128)} %bitcast.26), calls=%async_computation | async-start | bytes 131072 | tf_op jit(solution)/shard_map/all_to_all | solution.py:86
  344.4 9.2 %copy-start.3 = (f32[512,256]{1,0:T(8,128)S(1)}, f32[512,256]{1,0:T(8,128)}, u32[]{:S(2)}) copy-start(f32[512,256]{1,0:T(8,128)} %slice.133) | copy-start | bytes 1572868
  344.4 9.2 %copy-start.4 = (f32[512,256]{1,0:T(8,128)S(1)}, f32[512,256]{1,0:T(8,128)}, u32[]{:S(2)}) copy-start(f32[512,256]{1,0:T(8,128)} %fusion.12) | copy-start | bytes 1572868
  344.4 10.4 %copy-start.5 = (f32[256,256]{1,0:T(8,128)S(1)}, f32[256,256]{1,0:T(8,128)}, u32[]{:S(2)}) copy-start(f32[256,256]{1,0:T(8,128)} %get-tuple-element.51) | copy-start | bytes 786436
  344.4 264.6 %all-to-all-start.1 = ((f32[128,2,16384]{2,1,0:T(2,128)}), f32[128,2,16384]{2,1,0:T(2,128)}, u32[]{:S(2)}, u32[]{:S(2)}) async-start(f32[128,2,16384]{2,1,0:T(2,128)} %reshape.216), calls=%async_computation.1 | async-start | bytes 33554432 | tf_op jit(solution)/shard_map/all_to_all | solution.py:85
  629.5 33.5 %copy-start.1 = (s32[1,160,128]{2,1,0:T(8,128)S(1)}, s32[1,160,128]{2,1,0:T(8,128)}, u32[]{:S(2)}) copy-start(s32[1,160,128]{2,1,0:T(8,128)} %param.12) | copy-start | bytes 245764
Sparse Core Ops, SparseCore 0:
  76.1 73.0 all-gather.2
  151.9 71.1 all-gather.4
where the time goes:
time: 680 us; the launch traced here: 670 us
  waiting for transfers between devices  291 us (43%)
  matrix products  124 us (18%)
  other arithmetic  115 us (17%)
  local copies, waits for them, and re-layouts  94 us (14%)
  starting transfers between devices  20.1 us (3%)
  between operations  17.6 us (3%)
  loops' own time  8.6 us (1%)
    all_to_all x1, waiting for transfers between devices, body(): lax.all_to_all(outgoing, ('front', 'grid'), split_axis=0, concat_axis=0,...  252 us
    dot_general x2, matrix products, subtract_outer(): jnp.einsum('rk,ck->rc', left_rows, piece, precision=precise)  60.6 us
    all_gather x2, waiting for transfers between devices, body(): lax.all_gather(panel_cols, 'grid', axis=0, tiled=True)  39.6 us
    reshape x2, local copies, waits for them, and re-layouts, body(): arrived = arrived.reshape(devices * capacity, BLK * BLK)  38 us
    another operation x7, other arithmetic, factor_panels(): second_factor = jnp.linalg.cholesky(updated_pivot)  34.6 us
    another operation x6, other arithmetic, factor_panels(): first_factor = jnp.linalg.cholesky(corner[:NB, :NB])  34 us
    dot_general x1, matrix products, body(): moved = jnp.einsum('qrs,qsx->qrx', permuter, picked, precision=precise)  26.6 us
    unnamed x23, local copies, waits for them, and re-layouts  21.7 us
  transfers between devices with their start and end apart: 4, of which 2 were waited for; matrix products, arithmetic and copies ran while one was open for 32% of the time, Pallas kernels for 0%

commit v1 on v0

--- a/solution.py
+++ b/solution.py
@@ -2,6 +2,7 @@
 import jax.numpy as jnp
 from jax import lax
 from jax.sharding import PartitionSpec as P
+from jax.lax import all_to_all, axis_size
 
 BLK = 128
 NB = 256
@@ -37,9 +38,19 @@
     schur_rows = local_rows
     for column_start in (0, NB):
         panel_cols = border_factor[:, column_start : column_start + NB]
-        schur_rows = subtract_outer(
-            schur_rows, panel_cols, lax.all_gather(panel_cols, "grid", axis=0, tiled=True)
-        )
+
+        def spread_tokens(dimension_no, local_values):
+            return jnp.concatenate(
+                all_to_all(
+                    jnp.stack([local_values for _ in range(axis_size("grid"))], axis=0),
+                    "grid",
+                    0,
+                    0,
+                ),
+                axis=dimension_no,
+            )
+
+        schur_rows = subtract_outer(schur_rows, panel_cols, spread_tokens(0, panel_cols))
     group_size = lax.axis_size("grid")
     member = lax.axis_index("grid")
     per_dev = local_rows.shape[0] // BLK

time: 680 us -> 800 us (1.18)
  waiting for transfers between devices: 291 us -> 384 us
  starting transfers between devices: 20.1 us -> 43 us
  between operations: 17.6 us -> 4.2 us
  other arithmetic: 115 us -> 125 us
  local copies, waits for them, and re-layouts: 94 us -> 103 us
  loops' own time: 8.6 us -> 0.36 us
    all_to_all x0 -> x2, waiting for transfers between devices: none -> 133 us  [spread_tokens(): all_to_all(jnp.stack([local_values for _ in range(axis_size('grid'))], ax...]
    all_gather x2 -> x0, waiting for transfers between devices: 39.6 us -> none  [body(): lax.all_gather(panel_cols, 'grid', axis=0, tiled=True)]
    all_to_all x0 -> x2, starting transfers between devices: none -> 16.4 us  [spread_tokens(): all_to_all(jnp.stack([local_values for _ in range(axis_size('grid'))], ax...]
    another operation x2, other arithmetic: 19.7 us -> 29.7 us  [factor_panels(): jax.scipy.linalg.solve_triangular(second_factor, updated_border.T, lower=...]
    another operation x1, loops' own time: 8.29 us -> 0.05 us  [factor_panels(): jax.scipy.linalg.solve_triangular(second_factor, updated_border.T, lower=...]
    another operation x17 -> x19, local copies, waits for them, and re-layouts: 7.95 us -> 15.9 us  [the longest x2 8.05 us: spread_tokens(): jnp.stack([local_values for _ in range(axis_size('grid'))], axis=0)]
  transfers between devices with their start and end apart: 4 -> 4, of which waited for: 2 -> 3; matrix products, arithmetic and copies ran while one was open for 32% -> 29% of each run, Pallas kernels for 0% -> 0%
where the time goes in v1:
time: 800 us; the launch traced here: 790 us
  waiting for transfers between devices  384 us (48%)
  matrix products  131 us (16%)
  other arithmetic  125 us (16%)
  local copies, waits for them, and re-layouts  103 us (13%)
  starting transfers between devices  43 us (5%)
    all_to_all x1, waiting for transfers between devices, body(): lax.all_to_all(outgoing, ('front', 'grid'), split_axis=0, concat_axis=0,...  252 us
    all_to_all x2, waiting for transfers between devices, spread_tokens(): all_to_all(jnp.stack([local_values for _ in range(axis_size('grid'))], ax...  133 us
    dot_general x2, matrix products, subtract_outer(): jnp.einsum('rk,ck->rc', left_rows, piece, precision=precise)  60.4 us
    reshape x2, local copies, waits for them, and re-layouts, body(): arrived = arrived.reshape(devices * capacity, BLK * BLK)  38 us
    another operation x7, other arithmetic, factor_panels(): second_factor = jnp.linalg.cholesky(updated_pivot)  34.6 us
    another operation x6, other arithmetic, factor_panels(): first_factor = jnp.linalg.cholesky(corner[:NB, :NB])  34 us
    another operation x2, other arithmetic, factor_panels(): jax.scipy.linalg.solve_triangular(second_factor, updated_border.T, lower=...  29.7 us
    dot_general x1, matrix products, body(): moved = jnp.einsum('qrs,qsx->qrx', permuter, picked, precision=precise)  26.6 us
  transfers between devices with their start and end apart: 4, of which 3 were waited for; matrix products, arithmetic and copies ran while one was open for 29% of the time, Pallas kernels for 0%

profile of v1, /device:TPU:5, one launch (start us, length us, event | category | flops | bytes accessed | tf_op | source)
XLA Modules:
  0.0 790.5 jit_solution(1988943567327341436)
XLA Ops:
  0.7 1.6 copy.53
  3.2 11.7 %cholesky.130 = f32[128,128]{1,0:T(8,128)S(1)} custom-call(f32[128,128]{1,0:T(8,128)S(1)} %cholesky.194), custom_call_target="Cholesky" | custom-call | tf_op jit(solution)/shard_map/jit(cholesky)/cholesky | solution.py:14
  14.9 9.8 %custom-call.19 = f32[1,128,128]{1,2,0:T(8,128)S(1)} custom-call(f32[1,128,128]{2,1,0:T(8,128)S(1)} %get-tuple-element.65), custom_call_target="InvertDiagBlocksLowerTriangular" | custom-call | tf_op jit(solution)/shard_map/jit(cholesky)/cholesky | solution.py:14
  25.3 11.7 %cholesky.147 = f32[128,128]{1,0:T(8,128)S(1)} custom-call(f32[128,128]{1,0:T(8,128)S(1)} %convolution_subtract_fusion.5), custom_call_target="Cholesky" | custom-call | tf_op jit(solution)/shard_map/jit(cholesky)/cholesky | solution.py:14
  39.8 4.1 while.2
  40.6 1.3 bitcast_dynamic-update-slice_fusion.4
  42.6 1.3 bitcast_dynamic-update-slice_fusion.4
  43.9 19.7 %custom-call.16 = f32[2,128,128]{1,2,0:T(8,128)S(1)} custom-call(f32[2,128,128]{2,1,0:T(8,128)S(1)} %get-tuple-element.11), custom_call_target="InvertDiagBlocksLowerTriangular" | custom-call | tf_op jit(solution)/shard_map/jit(_solve_triangular)/triangular_solve | solution.py:16
  63.6 1.6 copy.55
  65.2 1.0 maximum_bitcast_fusion.1
  66.7 2.1 convolution_subtract_fusion.1
  68.9 1.8 fusion.37
  70.9 4.0 stack.4
  74.9 6.9 all-to-all-start.1
  81.8 1.1 convolution_subtract_fusion.3
  82.9 1.1 copy.59
  84.0 1.0 fusion.17
  85.0 11.7 %cholesky.164 = f32[128,128]{1,0:T(8,128)S(1)} custom-call(f32[128,128]{1,0:T(8,128)S(1)} %cholesky.197), custom_call_target="Cholesky" | custom-call | tf_op jit(solution)/shard_map/jit(cholesky)/cholesky | solution.py:21
  96.7 9.8 %custom-call.20 = f32[1,128,128]{1,2,0:T(8,128)S(1)} custom-call(f32[1,128,128]{2,1,0:T(8,128)S(1)} %get-tuple-element.61), custom_call_target="InvertDiagBlocksLowerTriangular" | custom-call | tf_op jit(solution)/shard_map/jit(cholesky)/cholesky | solution.py:21
  107.3 11.7 %cholesky.181 = f32[128,128]{1,0:T(8,128)S(1)} custom-call(f32[128,128]{1,0:T(8,128)S(1)} %convolution_subtract_fusion.4), custom_call_target="Cholesky" | custom-call | tf_op jit(solution)/shard_map/jit(cholesky)/cholesky | solution.py:21
  122.4 4.0 while.3
  123.0 1.4 bitcast_dynamic-update-slice_fusion.5
  124.9 1.4 bitcast_dynamic-update-slice_fusion.5
  126.3 29.0 %custom-call.17 = f32[2,128,128]{1,2,0:T(8,128)} custom-call(f32[2,128,128]{2,1,0:T(8,128)S(1)} %get-tuple-element.19), custom_call_target="InvertDiagBlocksLowerTriangular" | custom-call | tf_op jit(solution)/shard_map/jit(_solve_triangular)/triangular_solve | solution.py:22
  156.8 1.3 fusion.15
  158.2 1.3 convolution_subtract_fusion.2
  159.5 1.4 fusion.33
  161.0 39.9 %all-to-all-done.1 = f32[16,512,256]{2,1,0:T(8,128)} async-done(((f32[16,512,256]{2,1,0:T(8,128)}), f32[16,512,256]{2,1,0:T(8,128)}, u32[]{:S(2)}, u32[]{:S(2)}) %all-to-all-start.1) | async-done | bytes 8388640 | tf_op jit(solution)/shard_map/all_to_all | solution.py:44
  200.8 4.0 stack.5
  204.8 9.5 %all-to-all-start.2 = ((f32[16,512,256]{2,1,0:T(8,128)}), f32[16,512,256]{2,1,0:T(8,128)}, u32[]{:S(2)}, u32[]{:S(2)}) async-start(f32[16,512,256]{2,1,0:T(8,128)} %stack.5), calls=%async_computation.2 | async-start | bytes 16777216 | tf_op jit(solution)/shard_map/all_to_all | solution.py:44
  216.3 1.9 gather_fusion
  219.6 18.5 %fusion.56 = f32[512,8192]{1,0:T(8,128)} fusion(f32[8192,256]{1,0:T(8,128)} %bitcast.33, f32[768,256]{1,0:T(8,128)S(1)} %maximum_bitcast_fusion.2), kind=kOutput, calls=%fused_computation.134 | convolution fusion | flops 12884901888 | bytes 25690112 | tf_op jit(solution)/shard_map/rk,ck->rc/dot_general | solution.py:32
  238.1 92.8 %all-to-all-done.2 = f32[16,512,256]{2,1,0:T(8,128)} async-done(((f32[16,512,256]{2,1,0:T(8,128)}), f32[16,512,256]{2,1,0:T(8,128)}, u32[]{:S(2)}, u32[]{:S(2)}) %all-to-all-start.2) | async-done | bytes 8388640 | tf_op jit(solution)/shard_map/all_to_all | solution.py:44
  330.9 15.9 %all-to-all-start = ((s32[128,1,2]{2,1,0:T(1,128)}), s32[128,1,2]{2,1,0:T(1,128)S(1)}, u32[]{:S(2)}, u32[]{:S(2)}) async-start(s32[128,1,2]{2,1,0:T(1,128)} %bitcast.26), calls=%async_computation | async-start | bytes 131072 | tf_op jit(solution)/shard_map/all_to_all | solution.py:97
  346.8 41.9 %fusion.3 = f32[64,8,64,128]{3,1,2,0:T(8,128)} fusion(f32[512,8192]{1,0:T(8,128)} %fusion.56, f32[1,512,8192]{2,1,0:T(8,128)} %param.9, f32[8192,256]{1,0:T(8,128)} %bitcast.34, f32[128,512]{0,1:T(8,128)S(1)} %fusion.33, f32[128,512]{0,1:T(8,128)S(1)} %copy.62), kind=kOutput, calls=%fused_computation.10 | convolution fusion | flops 12893421568 | bytes 59244544 | tf_op jit(solution)/shard_map/rk,ck->rc/dot_general | solution.py:32
  388.7 14.1 %copy.76 = f32[64,8,64,128]{3,2,1,0:T(8,128)} copy(f32[64,8,64,128]{3,1,2,0:T(8,128)} %fusion.3) | data formatting | bytes 33554432
  402.9 20.7 %fusion.6 = f32[256,128,128]{2,0,1:T(8,128)S(1)} fusion(f32[256,4,64,1]{0,2,3,1:T(8,128)S(1)} %bitcast.142, f32[4,128,64,128]{3,2,1,0:T(8,128)} %bitcast.132), kind=kOutput, calls=%fused_computation.14 | convolution fusion | flops 12884901888 | bytes 33816576 | tf_op jit(solution)/shard_map/qkc,krcs->qrs/dot_general | solution.py:87
  423.6 26.6 %fusion.4 = f32[256,128,128]{2,1,0:T(8,128)} fusion(f32[256,128,128]{2,0,1:T(8,128)S(1)} %fusion.6, s32[256,128]{1,0:T(8,128)S(1)} %gather_fusion.1), kind=kOutput, calls=%fused_computation.11 | convolution fusion | flops 6446645248 | bytes 33685504 | tf_op jit(solution)/shard_map/qrs,qsx->qrx/dot_general | solution.py:92
  450.2 19.8 %reshape.228 = f32[128,2,16384]{2,1,0:T(2,128)} reshape(f32[256,128,128]{2,1,0:T(8,128)} %fusion.4) | data formatting | bytes 33554432 | tf_op jit(solution)/shard_map/reshape | solution.py:93
  469.9 10.7 %all-to-all-start.3 = ((f32[128,2,16384]{2,1,0:T(2,128)}), f32[128,2,16384]{2,1,0:T(2,128)}, u32[]{:S(2)}, u32[]{:S(2)}) async-start(f32[128,2,16384]{2,1,0:T(2,128)} %reshape.228), calls=%async_computation.3 | async-start | bytes 33554432 | tf_op jit(solution)/shard_map/all_to_all | solution.py:96
  480.7 1.1 maximum_bitcast_fusion
  481.8 1.1 fusion.11
  483.4 0.8 reduce.13
  484.3 251.7 %all-to-all-done.3 = f32[128,2,16384]{2,1,0:T(2,128)} async-done(((f32[128,2,16384]{2,1,0:T(2,128)}), f32[128,2,16384]{2,1,0:T(2,128)}, u32[]{:S(2)}, u32[]{:S(2)}) %all-to-all-start.3) | async-done | bytes 16777248 | tf_op jit(solution)/shard_map/all_to_all | solution.py:96
  736.1 20.5 %reshape.229 = f32[256,16384]{1,0:T(8,128)} reshape(f32[128,2,16384]{2,1,0:T(2,128)} %all-to-all-done.3) | data formatting | bytes 33554432 | tf_op jit(solution)/shard_map/reshape | solution.py:99
  756.6 17.5 %copy.69 = f32[256,16384]{0,1:T(8,128)} copy(f32[256,16384]{1,0:T(8,128)} %reshape.229) | data formatting | bytes 33554432 | tf_op jit(solution)/shard_map/reshape | solution.py:99
  774.1 11.4 %fusion.43 = f32[64,128,128]{2,0,1:T(8,128)S(1)} fusion(f32[128,128,256]{2,1,0:T(8,128)} %bitcast.131, s32[256]{0:T(256)S(1)} %eq.86), kind=kOutput, calls=%fused_computation.86 | convolution fusion | flops 3221241856 | bytes 20972544 | tf_op jit(solution)/shard_map/rs,rx->sx/dot_general | solution.py:102
  785.6 4.4 copy.70
  (88 shorter events, 14.4 us)
Async XLA Ops:
  0.6 214.9 %copy-start = (s32[1,160,128]{2,1,0:T(8,128)S(1)}, s32[1,160,128]{2,1,0:T(8,128)}, u32[]{:S(2)}) copy-start(s32[1,160,128]{2,1,0:T(8,128)} %param.12) | copy-start | bytes 245764
  43.9 21.3 %copy-start.4 = (f32[256,256]{1,0:T(8,128)}, f32[256,256]{1,0:T(8,128)S(1)}, u32[]{:S(2)}) copy-start(f32[256,256]{1,0:T(8,128)S(1)} %get-tuple-element.164) | copy-start | bytes 786436
  74.9 125.9 %all-to-all-start.1 = ((f32[16,512,256]{2,1,0:T(8,128)}), f32[16,512,256]{2,1,0:T(8,128)}, u32[]{:S(2)}, u32[]{:S(2)}) async-start(f32[16,512,256]{2,1,0:T(8,128)} %stack.4), calls=%async_computation.1 | async-start | bytes 16777216 | tf_op jit(solution)/shard_map/all_to_all | solution.py:44
  107.0 107.4 %copy-start.7 = (s32[1,160,1]{1,2,0:T(1,128)S(1)}, s32[1,160,1]{1,2,0:T(1,128)}, u32[]{:S(2)}) copy-start(s32[1,160,1]{1,2,0:T(1,128)} %param.10) | copy-start | bytes 1924
  126.3 89.9 %copy-start.2 = (s32[1,160]{1,0:T(1,128)S(1)}, s32[1,160]{1,0:T(1,128)}, u32[]{:S(2)}) copy-start(s32[1,160]{1,0:T(1,128)} %param.11) | copy-start | bytes 1924
  156.0 0.8 copy-start.3
  204.8 126.1 %all-to-all-start.2 = ((f32[16,512,256]{2,1,0:T(8,128)}), f32[16,512,256]{2,1,0:T(8,128)}, u32[]{:S(2)}, u32[]{:S(2)}) async-start(f32[16,512,256]{2,1,0:T(8,128)} %stack.5), calls=%async_computation.2 | async-start | bytes 16777216 | tf_op jit(solution)/shard_map/all_to_all | solution.py:44
  330.9 139.0 %all-to-all-start = ((s32[128,1,2]{2,1,0:T(1,128)}), s32[128,1,2]{2,1,0:T(1,128)S(1)}, u32[]{:S(2)}, u32[]{:S(2)}) async-start(s32[128,1,2]{2,1,0:T(1,128)} %bitcast.26), calls=%async_computation | async-start | bytes 131072 | tf_op jit(solution)/shard_map/all_to_all | solution.py:97
  469.9 11.8 %copy-start.5 = (f32[256,256]{1,0:T(8,128)S(1)}, f32[256,256]{1,0:T(8,128)}, u32[]{:S(2)}) copy-start(f32[256,256]{1,0:T(8,128)} %get-tuple-element.51) | copy-start | bytes 786436
  469.9 11.8 %copy-start.6 = (f32[256,256]{1,0:T(8,128)S(1)}, f32[256,256]{1,0:T(8,128)}, u32[]{:S(2)}) copy-start(f32[256,256]{1,0:T(8,128)} %get-tuple-element.49) | copy-start | bytes 786436
  469.9 266.1 %all-to-all-start.3 = ((f32[128,2,16384]{2,1,0:T(2,128)}), f32[128,2,16384]{2,1,0:T(2,128)}, u32[]{:S(2)}, u32[]{:S(2)}) async-start(f32[128,2,16384]{2,1,0:T(2,128)} %reshape.228), calls=%async_computation.3 | async-start | bytes 33554432 | tf_op jit(solution)/shard_map/all_to_all | solution.py:96
  756.6 33.4 %copy-start.1 = (s32[1,160,128]{2,1,0:T(8,128)S(1)}, s32[1,160,128]{2,1,0:T(8,128)}, u32[]{:S(2)}) copy-start(s32[1,160,128]{2,1,0:T(8,128)} %param.12) | copy-start | bytes 245764
